TPU v7x, 32 devices: a whole 2x2x4 slice. The times are simulated.
32 devices in a mesh: src: 4 (over x, core), dst: 2 (over y), tm: 4 (over z).
Axes of the slice: x: 2, y: 2, z: 4, core: 2. Of those that a mesh axis runs over, the one named last changes fastest.
Arguments:
- traffic: bfloat16 [256, 256, 512], P('src', 'dst', 'tm'), may hold values from -6 to 6
- src_factor: float32 [256, 64], P('src'), may hold values from -0.75 to 0.75
- dst_factor: float32 [256, 64], P('dst'), may hold values from -0.75 to 0.75
- time_factor: float32 [512, 64], P('tm'), may hold values from -0.75 to 0.75
Outputs:
- grad_src: float32 [256, 64], P('src')
- grad_dst: float32 [256, 64], P('dst')
- grad_time: float32 [512, 64], P('tm')
All inputs are finite; a program needn't handle non-finite values.
Results may differ from a plain program's by a relative error of at most 0.0003.
Values sent between devices are 32-bit elements; how exact they have to be, the bound alone decides.
No kernel may reach another device: no remote copies, remote signals or barrier semaphores. Data moves between devices by JAX's collectives and lax.ppermute only.
A program may use at most 64 MiB of HBM per device.

v0:
```python
import jax
import jax.numpy as jnp
from jax import lax
from jax.sharding import PartitionSpec as P

DAY = 288
STEPS = 3
hour_weight = 32.0
day_weight = 64.0
step_rate = 0.1
highest = lax.Precision.HIGHEST


def passed_along(block, axis, distance):
    devices = range(lax.axis_size(axis))
    route = [(i - distance, i) for i in devices if i - distance in devices]
    return lax.ppermute(block, axis, route)


def behind(values, offset):
    row_count = values.shape[0]
    whole_blocks, extra_rows = divmod(offset, row_count)
    pieces = []
    for part_by, first_row, last_row in (
        (whole_blocks + 1, row_count - extra_rows, row_count),
        (whole_blocks, 0, row_count - extra_rows),
    ):
        block_rows = values[first_row:last_row]
        if part_by == 0:
            pieces.append(block_rows)
        else:
            pieces.append(passed_along(block_rows, "tm", part_by))
    return jnp.concatenate(pieces, 0)


def ahead(values, offset):
    row_count = values.shape[0]
    whole_blocks, extra_rows = divmod(offset, row_count)
    pieces = []
    for part_by, first_row, last_row in (
        (-whole_blocks, extra_rows, row_count),
        (-(whole_blocks + 1), 0, extra_rows),
    ):
        block_rows = values[first_row:last_row]
        if part_by == 0:
            pieces.append(block_rows)
        else:
            pieces.append(passed_along(block_rows, "tm", part_by))
    return jnp.concatenate(pieces, 0)


def smoothing(time_now, position):
    hour_diff = jnp.where((position >= 1)[:, None], time_now - behind(time_now, 1), 0.0)
    day_diff = jnp.where((position >= DAY)[:, None], time_now - behind(time_now, DAY), 0.0)
    hour_next = ahead(hour_diff, 1)
    day_next = ahead(day_diff, DAY)
    return hour_weight * (hour_diff - hour_next) + day_weight * (day_diff - day_next)


def on_device(traffic, src_factor, dst_factor, time_factor):
    src_rows, rank_count = src_factor.shape
    dst_rows = dst_factor.shape[0]
    time_rows = time_factor.shape[0]
    position = lax.axis_index("tm") * time_rows + jnp.arange(time_rows, dtype=jnp.int32)
    observed = traffic.reshape(src_rows, dst_rows * time_rows)
    src_now, dst_now, time_now = (src_factor, dst_factor, time_factor)
    for iteration in range(STEPS):
        dst_time = (dst_now.T[:, :, None] * time_now.T[:, None, :]).reshape(
            rank_count, dst_rows * time_rows
        )
        model_cells = jnp.dot(src_now, dst_time, precision=highest)
        residual = model_cells - observed.astype(jnp.float32)
        raw_src = jnp.einsum("ix,rx->ir", residual, dst_time, precision=highest)
        resid_cube = residual.reshape(src_rows, dst_rows, time_rows)
        src_time = src_now.T[:, :, None] * time_now.T[:, None, :]
        raw_dst = jnp.einsum("ijk,rik->jr", resid_cube, src_time, precision=highest)
        src_dst = src_now.T[:, :, None] * dst_now.T[:, None, :]
        raw_time = jnp.einsum("ijk,rij->kr", resid_cube, src_dst, precision=highest)
        grad_src = lax.psum(raw_src, ("dst", "tm")) / rank_count
        grad_dst = lax.psum(raw_dst, ("src", "tm")) / rank_count
        summed_time = lax.psum(raw_time, ("src", "dst"))
        grad_time = (summed_time + smoothing(time_now, position)) / rank_count
        if iteration + 1 < STEPS:
            src_now = src_now - step_rate * grad_src
            dst_now = dst_now - step_rate * grad_dst
            time_now = time_now - step_rate * grad_time
    return (grad_src, grad_dst, grad_time)


def solution(mesh):
    in_specs = (P("src", "dst", "tm"), P("src", None), P("dst", None), P("tm", None))
    out_specs = (P("src", None), P("dst", None), P("tm", None))
    return jax.shard_map(
        on_device, mesh=mesh, in_specs=in_specs, out_specs=out_specs, check_vma=False
    )
```

profile of v0, /device:TPU:27, one launch (start us, length us, event | category | flops | bytes accessed | tf_op | source)
XLA Modules:
  0.0 477.5 jit_solution(11695391213092118398)
XLA Ops:
  0.7 0.9 slice.72
  1.5 1.3 collective-permute-start
  2.8 0.8 slice.76
  3.7 1.3 collective-permute-start.2
  5.0 1.3 collective-permute-start.3
  6.3 2.1 convert.1
  8.4 1.2 broadcast_multiply_fusion.2
  9.6 8.5 %fusion = f32[64,16384]{1,0:T(8,128)S(1)} fusion(f32[64,64]{1,0:T(8,128)S(1)} %copy-done.4, f32[8,8,128,128]{3,2,1,0:T(8,128)S(1)} %bitcast.86, f32[8,8,128,128]{3,2,1,0:T(8,128)S(1)} %convert.1), kind=kOutput, calls=%fused_computation.3 | convolution fusion | flops 806354944 | bytes 12599296 | tf_op jit(solution)/shard_map/dot_general | solution.py:71
  18.1 14.4 %fusion.7 = f32[64,64]{1,0:T(8,128)S(1)} fusion(f32[64,16384]{1,0:T(8,128)S(1)} %fusion, f32[8,8,128,128]{3,2,1,0:T(8,128)S(1)} %bitcast.87), kind=kOutput, calls=%fused_computation.10 | convolution fusion | flops 805306368 | bytes 8404992 | tf_op jit(solution)/shard_map/ix,rx->ir/dot_general | solution.py:73
  32.6 0.7 copy.9
  33.3 2.9 fusion.31
  36.3 4.5 fusion.28
  40.7 26.9 %psum.63 = f32[64,64]{1,0:T(8,128)S(1)} all-reduce(f32[64,64]{1,0:T(8,128)S(1)} %fusion.7), channel_id=1, replica_groups=mesh['src'=4,'dst'=2,'tm'=4] {'dst','tm'}, use_global_device_ids=true, to_apply=%region_0.0 | all-reduce | flops 4096 | bytes 32768 | tf_op jit(solution)/shard_map/psum | solution.py:79
  67.7 64.5 %psum.64 = f32[128,64]{0,1:T(8,128)S(1)} all-reduce(f32[128,64]{0,1:T(8,128)S(1)} %fusion.28), channel_id=1, replica_groups=mesh['src'=4,'dst'=2,'tm'=4] {'src','tm'}, use_global_device_ids=true, to_apply=%region_1.0 | all-reduce | flops 8192 | bytes 65536 | tf_op jit(solution)/shard_map/psum | solution.py:80
  132.4 1.7 collective-permute-start.4
  134.1 4.0 collective-permute-start.1
  138.1 1.3 collective-permute-start.5
  139.4 27.7 %psum.65 = f32[128,64]{0,1:T(8,128)S(1)} all-reduce(f32[128,64]{0,1:T(8,128)S(1)} %fusion.31), channel_id=1, replica_groups=mesh['src'=4,'dst'=2,'tm'=4] {'src','dst'}, use_global_device_ids=true, to_apply=%region_2.0 | all-reduce | flops 8192 | bytes 65536 | tf_op jit(solution)/shard_map/psum | solution.py:81
  167.5 1.2 broadcast_multiply_fusion.1
  169.3 8.1 %convolution_subtract_fusion.1 = f32[64,16384]{1,0:T(8,128)S(1)} fusion(f32[64,64]{1,0:T(8,128)S(1)} %multiply_subtract_fusion.2, f32[8,8,128,128]{3,2,1,0:T(8,128)S(1)} %bitcast.88, f32[8,8,128,128]{3,2,1,0:T(8,128)S(1)} %copy-done.1), kind=kOutput, calls=%fused_computation.1 | convolution fusion | flops 806354944 | bytes 12599296 | tf_op jit(solution)/shard_map/dot_general | solution.py:71
  177.4 6.0 %fusion.4 = f32[64,64]{1,0:T(8,128)S(1)} fusion(f32[64,16384]{1,0:T(8,128)S(1)} %convolution_subtract_fusion.1, f32[8,8,128,128]{3,2,1,0:T(8,128)S(1)} %bitcast.89), kind=kOutput, calls=%fused_computation.7 | convolution fusion | flops 805306368 | bytes 8404992 | tf_op jit(solution)/shard_map/ix,rx->ir/dot_general | solution.py:73
  183.5 0.7 copy.11
  184.2 2.9 fusion.37
  187.2 4.5 fusion.34
  191.6 1.3 collective-permute-start.6
  192.9 1.3 collective-permute-start.8
  194.2 1.3 collective-permute-start.9
  195.5 58.0 %psum.67 = f32[128,64]{0,1:T(8,128)S(1)} all-reduce(f32[128,64]{0,1:T(8,128)S(1)} %fusion.34), channel_id=1, replica_groups=mesh['src'=4,'dst'=2,'tm'=4] {'src','tm'}, use_global_device_ids=true, to_apply=%region_4.5 | all-reduce | flops 8192 | bytes 65536 | tf_op jit(solution)/shard_map/psum | solution.py:80
  253.5 25.8 %psum.66 = f32[64,64]{1,0:T(8,128)S(1)} all-reduce(f32[64,64]{1,0:T(8,128)S(1)} %fusion.4), channel_id=1, replica_groups=mesh['src'=4,'dst'=2,'tm'=4] {'dst','tm'}, use_global_device_ids=true, to_apply=%region_3.4 | all-reduce | flops 4096 | bytes 32768 | tf_op jit(solution)/shard_map/psum | solution.py:79
  279.5 1.5 collective-permute-start.10
  281.0 6.3 %collective-permute-start.7 = (f32[1,64]{0,1:T(8,128)S(1)}, f32[1,64]{0,1:T(8,128)S(1)}, u32[]{:S(2)}, u32[]{:S(2)}) collective-permute-start(f32[1,64]{0,1:T(8,128)S(1)} %bitcast.116), channel_id=1, source_target_pairs={{1,0},{2,1},{3,2},{5,4},{6,5},{7,6},{9,8},{10,9},{11,10},{13,12},{... | collective-permute-start | bytes 776 | tf_op jit(solution)/shard_map/ppermute | solution.py:17
  287.3 1.3 collective-permute-start.11
  288.6 32.4 %psum.68 = f32[128,64]{0,1:T(8,128)S(1)} all-reduce(f32[128,64]{0,1:T(8,128)S(1)} %fusion.37), channel_id=1, replica_groups=mesh['src'=4,'dst'=2,'tm'=4] {'src','dst'}, use_global_device_ids=true, to_apply=%region_5.6 | all-reduce | flops 8192 | bytes 65536 | tf_op jit(solution)/shard_map/psum | solution.py:81
  321.4 1.2 broadcast_multiply_fusion
  323.2 8.1 %convolution_subtract_fusion = f32[64,16384]{1,0:T(8,128)S(1)} fusion(f32[8,8,128,128]{3,2,1,0:T(8,128)S(1)} %bitcast.82, f32[8,8,128,128]{3,2,1,0:T(8,128)S(1)} %copy-done.2, f32[64,64]{1,0:T(8,128)S(1)} %multiply_subtract_fusion.2, f32[64,64]{1,0:T(8,128)S(1)} %psum.66), kind=kOutput, calls=%fused_computation | convolution fusion | flops 806363136 | bytes 12615680 | tf_op jit(solution)/shard_map/dot_general | solution.py:71
  331.3 5.8 %fusion.1 = f32[64,64]{1,0:T(8,128)S(1)} fusion(f32[64,16384]{1,0:T(8,128)S(1)} %convolution_subtract_fusion, f32[8,8,128,128]{3,2,1,0:T(8,128)S(1)} %bitcast.83), kind=kOutput, calls=%fused_computation.4 | convolution fusion | flops 805306368 | bytes 8404992 | tf_op jit(solution)/shard_map/ix,rx->ir/dot_general | solution.py:73
  337.2 0.7 copy.13
  338.0 2.9 fusion.43
  340.9 4.5 fusion.40
  345.4 1.3 collective-permute-start.12
  346.7 1.3 collective-permute-start.14
  348.0 1.3 collective-permute-start.15
  349.3 26.0 %psum.69 = f32[64,64]{1,0:T(8,128)S(1)} all-reduce(f32[64,64]{1,0:T(8,128)S(1)} %fusion.1), channel_id=1, replica_groups=mesh['src'=4,'dst'=2,'tm'=4] {'dst','tm'}, use_global_device_ids=true, to_apply=%region_6.7 | all-reduce | flops 4096 | bytes 32768 | tf_op jit(solution)/shard_map/psum | solution.py:79
  375.9 65.0 %psum.70 = f32[128,64]{0,1:T(8,128)S(1)} all-reduce(f32[128,64]{0,1:T(8,128)S(1)} %fusion.40), channel_id=1, replica_groups=mesh['src'=4,'dst'=2,'tm'=4] {'src','tm'}, use_global_device_ids=true, to_apply=%region_7.8 | all-reduce | flops 8192 | bytes 65536 | tf_op jit(solution)/shard_map/psum | solution.py:80
  441.1 1.8 collective-permute-start.16
  443.6 4.0 collective-permute-start.13
  447.5 1.3 collective-permute-start.17
  448.8 27.5 %psum.71 = f32[128,64]{0,1:T(8,128)S(1)} all-reduce(f32[128,64]{0,1:T(8,128)S(1)} %fusion.43), channel_id=1, replica_groups=mesh['src'=4,'dst'=2,'tm'=4] {'src','dst'}, use_global_device_ids=true, to_apply=%region_8.9 | all-reduce | flops 8192 | bytes 65536 | tf_op jit(solution)/shard_map/psum | solution.py:81
  (53 shorter events, 4.6 us)
Async XLA Ops:
  0.6 7.8 %copy-start.3 = (f32[128,64]{0,1:T(8,128)S(1)}, f32[128,64]{0,1:T(8,128)}, u32[]{:S(2)}) copy-start(f32[128,64]{0,1:T(8,128)} %param.7) | copy-start | bytes 98308
  0.6 7.8 %copy-start.5 = (f32[128,64]{0,1:T(8,128)S(1)}, f32[128,64]{0,1:T(8,128)}, u32[]{:S(2)}) copy-start(f32[128,64]{0,1:T(8,128)} %param.6) | copy-start | bytes 98308
  1.5 130.6 %collective-permute-start = (f32[1,64]{0,1:T(8,128)S(1)}, f32[1,64]{0,1:T(8,128)S(1)}, u32[]{:S(2)}, u32[]{:S(2)}) collective-permute-start(f32[1,64]{0,1:T(8,128)S(1)} %slice.72), channel_id=1, source_target_pairs={{0,1},{1,2},{2,3},{4,5},{5,6},{6,7},{8,9},{9,10},{10,11},{12,13},{... | collective-permute-start | bytes 776 | tf_op jit(solution)/shard_map/ppermute | solution.py:17
  3.7 128.5 %collective-permute-start.2 = (f32[32,64]{0,1:T(8,128)S(1)}, f32[32,64]{0,1:T(8,128)S(1)}, u32[]{:S(2)}, u32[]{:S(2)}) collective-permute-start(f32[32,64]{0,1:T(8,128)S(1)} %slice.76), channel_id=1, source_target_pairs={{0,3},{4,7},{8,11},{12,15},{16,19},{20,23},{24,27},{28,31}} | collective-permute-start | bytes 24584 | tf_op jit(solution)/shard_map/ppermute | solution.py:17
  5.0 127.2 %collective-permute-start.3 = (f32[96,64]{0,1:T(8,128)}, f32[96,64]{0,1:T(8,128)S(1)}, u32[]{:S(2)}, u32[]{:S(2)}) collective-permute-start(f32[96,64]{0,1:T(8,128)} %bitcast.101), channel_id=1, source_target_pairs={{0,2},{1,3},{4,6},{5,7},{8,10},{9,11},{12,14},{13,15},{16,18},{17,... | collective-permute-start | bytes 73736 | tf_op jit(solution)/shard_map/ppermute | solution.py:17
  6.3 3.3 copy-start.4
  8.4 9.7 %copy-start = (f32[8,8,128,128]{3,2,1,0:T(8,128)}, f32[8,8,128,128]{3,2,1,0:T(8,128)S(1)}, u32[]{:S(2)}) copy-start(f32[8,8,128,128]{3,2,1,0:T(8,128)S(1)} %convert.1) | copy-start | bytes 12582916
  132.4 34.9 %collective-permute-start.4 = (f32[96,64]{0,1:T(8,128)S(1)}, f32[96,64]{0,1:T(8,128)S(1)}, u32[]{:S(2)}, u32[]{:S(2)}) collective-permute-start(f32[96,64]{0,1:T(8,128)S(1)} %slice.98), channel_id=1, source_target_pairs={{2,0},{3,1},{6,4},{7,5},{10,8},{11,9},{14,12},{15,13},{18,16},{19,... | collective-permute-start | bytes 73736 | tf_op jit(solution)/shard_map/ppermute | solution.py:17
  134.1 33.1 %collective-permute-start.1 = (f32[1,64]{0,1:T(8,128)S(1)}, f32[1,64]{0,1:T(8,128)S(1)}, u32[]{:S(2)}, u32[]{:S(2)}) collective-permute-start(f32[1,64]{0,1:T(8,128)S(1)} %bitcast.118), channel_id=1, source_target_pairs={{1,0},{2,1},{3,2},{5,4},{6,5},{7,6},{9,8},{10,9},{11,10},{13,12},{... | collective-permute-start | bytes 776 | tf_op jit(solution)/shard_map/ppermute | solution.py:17
  138.1 29.1 %collective-permute-start.5 = (f32[32,64]{0,1:T(8,128)S(1)}, f32[32,64]{0,1:T(8,128)S(1)}, u32[]{:S(2)}, u32[]{:S(2)}) collective-permute-start(f32[32,64]{0,1:T(8,128)S(1)} %bitcast.117), channel_id=1, source_target_pairs={{3,0},{7,4},{11,8},{15,12},{19,16},{23,20},{27,24},{31,28}} | collective-permute-start | bytes 24584 | tf_op jit(solution)/shard_map/ppermute | solution.py:17
  167.1 2.2 copy-start.1
  191.6 87.7 %collective-permute-start.6 = (f32[1,64]{0,1:T(8,128)S(1)}, f32[1,64]{0,1:T(8,128)S(1)}, u32[]{:S(2)}, u32[]{:S(2)}) collective-permute-start(f32[1,64]{0,1:T(8,128)S(1)} %slice.100), channel_id=1, source_target_pairs={{0,1},{1,2},{2,3},{4,5},{5,6},{6,7},{8,9},{9,10},{10,11},{12,13},{... | collective-permute-start | bytes 776 | tf_op jit(solution)/shard_map/ppermute | solution.py:17
  192.9 86.4 %collective-permute-start.8 = (f32[32,64]{0,1:T(8,128)S(1)}, f32[32,64]{0,1:T(8,128)S(1)}, u32[]{:S(2)}, u32[]{:S(2)}) collective-permute-start(f32[32,64]{0,1:T(8,128)S(1)} %slice.104), channel_id=1, source_target_pairs={{0,3},{4,7},{8,11},{12,15},{16,19},{20,23},{24,27},{28,31}} | collective-permute-start | bytes 24584 | tf_op jit(solution)/shard_map/ppermute | solution.py:17
  194.2 85.1 %collective-permute-start.9 = (f32[96,64]{0,1:T(8,128)S(1)}, f32[96,64]{0,1:T(8,128)S(1)}, u32[]{:S(2)}, u32[]{:S(2)}) collective-permute-start(f32[96,64]{0,1:T(8,128)S(1)} %bitcast.98), channel_id=1, source_target_pairs={{0,2},{1,3},{4,6},{5,7},{8,10},{9,11},{12,14},{13,15},{16,18},{17,... | collective-permute-start | bytes 73736 | tf_op jit(solution)/shard_map/ppermute | solution.py:17
  279.5 41.6 %collective-permute-start.10 = (f32[96,64]{0,1:T(8,128)S(1)}, f32[96,64]{0,1:T(8,128)S(1)}, u32[]{:S(2)}, u32[]{:S(2)}) collective-permute-start(f32[96,64]{0,1:T(8,128)S(1)} %slice.106), channel_id=1, source_target_pairs={{2,0},{3,1},{6,4},{7,5},{10,8},{11,9},{14,12},{15,13},{18,16},{19,... | collective-permute-start | bytes 73736 | tf_op jit(solution)/shard_map/ppermute | solution.py:17
  281.0 40.1 %collective-permute-start.7 = (f32[1,64]{0,1:T(8,128)S(1)}, f32[1,64]{0,1:T(8,128)S(1)}, u32[]{:S(2)}, u32[]{:S(2)}) collective-permute-start(f32[1,64]{0,1:T(8,128)S(1)} %bitcast.116), channel_id=1, source_target_pairs={{1,0},{2,1},{3,2},{5,4},{6,5},{7,6},{9,8},{10,9},{11,10},{13,12},{... | collective-permute-start | bytes 776 | tf_op jit(solution)/shard_map/ppermute | solution.py:17
  287.3 33.8 %collective-permute-start.11 = (f32[32,64]{0,1:T(8,128)S(1)}, f32[32,64]{0,1:T(8,128)S(1)}, u32[]{:S(2)}, u32[]{:S(2)}) collective-permute-start(f32[32,64]{0,1:T(8,128)S(1)} %bitcast.115), channel_id=1, source_target_pairs={{3,0},{7,4},{11,8},{15,12},{19,16},{23,20},{27,24},{31,28}} | collective-permute-start | bytes 24584 | tf_op jit(solution)/shard_map/ppermute | solution.py:17
  321.0 2.2 copy-start.2
  345.4 95.6 %collective-permute-start.12 = (f32[1,64]{0,1:T(8,128)S(1)}, f32[1,64]{0,1:T(8,128)S(1)}, u32[]{:S(2)}, u32[]{:S(2)}) collective-permute-start(f32[1,64]{0,1:T(8,128)S(1)} %slice.108), channel_id=1, source_target_pairs={{0,1},{1,2},{2,3},{4,5},{5,6},{6,7},{8,9},{9,10},{10,11},{12,13},{... | collective-permute-start | bytes 776 | tf_op jit(solution)/shard_map/ppermute | solution.py:17
  346.7 94.3 %collective-permute-start.14 = (f32[32,64]{0,1:T(8,128)S(1)}, f32[32,64]{0,1:T(8,128)S(1)}, u32[]{:S(2)}, u32[]{:S(2)}) collective-permute-start(f32[32,64]{0,1:T(8,128)S(1)} %slice.112), channel_id=1, source_target_pairs={{0,3},{4,7},{8,11},{12,15},{16,19},{20,23},{24,27},{28,31}} | collective-permute-start | bytes 24584 | tf_op jit(solution)/shard_map/ppermute | solution.py:17
  348.0 93.0 %collective-permute-start.15 = (f32[96,64]{0,1:T(8,128)S(1)}, f32[96,64]{0,1:T(8,128)S(1)}, u32[]{:S(2)}, u32[]{:S(2)}) collective-permute-start(f32[96,64]{0,1:T(8,128)S(1)} %bitcast.107), channel_id=1, source_target_pairs={{0,2},{1,3},{4,6},{5,7},{8,10},{9,11},{12,14},{13,15},{16,18},{17,... | collective-permute-start | bytes 73736 | tf_op jit(solution)/shard_map/ppermute | solution.py:17
  441.1 35.3 %collective-permute-start.16 = (f32[96,64]{0,1:T(8,128)S(1)}, f32[96,64]{0,1:T(8,128)S(1)}, u32[]{:S(2)}, u32[]{:S(2)}) collective-permute-start(f32[96,64]{0,1:T(8,128)S(1)} %slice.114), channel_id=1, source_target_pairs={{2,0},{3,1},{6,4},{7,5},{10,8},{11,9},{14,12},{15,13},{18,16},{19,... | collective-permute-start | bytes 73736 | tf_op jit(solution)/shard_map/ppermute | solution.py:17
  443.6 32.9 %collective-permute-start.13 = (f32[1,64]{0,1:T(8,128)S(1)}, f32[1,64]{0,1:T(8,128)S(1)}, u32[]{:S(2)}, u32[]{:S(2)}) collective-permute-start(f32[1,64]{0,1:T(8,128)S(1)} %bitcast.120), channel_id=1, source_target_pairs={{1,0},{2,1},{3,2},{5,4},{6,5},{7,6},{9,8},{10,9},{11,10},{13,12},{... | collective-permute-start | bytes 776 | tf_op jit(solution)/shard_map/ppermute | solution.py:17
  447.5 28.9 %collective-permute-start.17 = (f32[32,64]{0,1:T(8,128)S(1)}, f32[32,64]{0,1:T(8,128)S(1)}, u32[]{:S(2)}, u32[]{:S(2)}) collective-permute-start(f32[32,64]{0,1:T(8,128)S(1)} %bitcast.119), channel_id=1, source_target_pairs={{3,0},{7,4},{11,8},{15,12},{19,16},{23,20},{27,24},{31,28}} | collective-permute-start | bytes 24584 | tf_op jit(solution)/shard_map/ppermute | solution.py:17
where the time goes:
time: 487 us; the launch traced here: 478 us
  blocking collectives  354 us (73%)
  matrix products  73.3 us (15%)
  starting transfers between devices  34.7 us (7%)
  other arithmetic  8.03 us (2%)
  local copies, waits for them, and re-layouts  6.05 us (1%)
    psum x3, blocking collectives, on_device(): grad_dst = lax.psum(raw_dst, ('src', 'tm')) / rank_count  187 us
    psum x3, blocking collectives, on_device(): summed_time = lax.psum(raw_time, ('src', 'dst'))  87.6 us
    psum x3, blocking collectives, on_device(): grad_src = lax.psum(raw_src, ('dst', 'tm')) / rank_count  78.8 us
    ppermute x18, starting transfers between devices, passed_along(): return lax.ppermute(block, axis, route)  34.7 us
    dot_general x3, matrix products, on_device(): raw_src = jnp.einsum('ix,rx->ir', residual, dst_time, precision=highest)  26.3 us
    dot_general x3, matrix products, on_device(): model_cells = jnp.dot(src_now, dst_time, precision=highest)  24.7 us
    dot_general x3, matrix products, on_device(): raw_dst = jnp.einsum('ijk,rik->jr', resid_cube, src_time, precision=highest)  13.4 us
  transfers between devices with their start and end apart: 18, of which 0 were waited for; matrix products, arithmetic and copies ran while one was open for 8% of the time, Pallas kernels for 0%

commit v1 on v0

--- a/solution.py
+++ b/solution.py
@@ -9,6 +9,10 @@
 day_weight = 64.0
 step_rate = 0.1
 highest = lax.Precision.HIGHEST
+
+
+def compute_the_numbers(local_array, bus_axis):
+    return jnp.sum(lax.all_gather(local_array, axis_name=bus_axis), axis=0)
 
 
 def passed_along(block, axis, distance):
@@ -76,7 +80,7 @@
         raw_dst = jnp.einsum("ijk,rik->jr", resid_cube, src_time, precision=highest)
         src_dst = src_now.T[:, :, None] * dst_now.T[:, None, :]
         raw_time = jnp.einsum("ijk,rij->kr", resid_cube, src_dst, precision=highest)
-        grad_src = lax.psum(raw_src, ("dst", "tm")) / rank_count
+        grad_src = compute_the_numbers(raw_src, ("dst", "tm")) / rank_count
         grad_dst = lax.psum(raw_dst, ("src", "tm")) / rank_count
         summed_time = lax.psum(raw_time, ("src", "dst"))
         grad_time = (summed_time + smoothing(time_now, position)) / rank_count

time: 487 us -> 473 us (0.971)
  matrix products: 73.3 us -> 64.7 us
  blocking collectives: 354 us -> 348 us
    psum x3 -> x0, blocking collectives: 78.8 us -> none  [on_device(): grad_src = lax.psum(raw_src, ('dst', 'tm')) / rank_count]
    all_gather x0 -> x3, blocking collectives: none -> 74.5 us  [compute_the_numbers(): return jnp.sum(lax.all_gather(local_array, axis_name=bus_axis), axis=0)]
    psum x3, blocking collectives: 187 us -> 174 us  [on_device(): grad_dst = lax.psum(raw_dst, ('src', 'tm')) / rank_count]
    psum x3, blocking collectives: 87.6 us -> 100 us  [on_device(): summed_time = lax.psum(raw_time, ('src', 'dst'))]
    dot_general x3, matrix products: 26.3 us -> 17.8 us  [on_device(): raw_src = jnp.einsum('ix,rx->ir', residual, dst_time, precision=highest)]
  transfers between devices with their start and end apart: 18 -> 18, of which waited for: 0 -> 0; matrix products, arithmetic and copies ran while one was open for 8% -> 6% of each run, Pallas kernels for 0% -> 0%
where the time goes in v1:
time: 473 us; the launch traced here: 463 us
  blocking collectives  348 us (74%)
  matrix products  64.7 us (14%)
  starting transfers between devices  34.4 us (7%)
  other arithmetic  8.1 us (2%)
  local copies, waits for them, and re-layouts  6.05 us (1%)
    psum x3, blocking collectives, on_device(): grad_dst = lax.psum(raw_dst, ('src', 'tm')) / rank_count  174 us
    psum x3, blocking collectives, on_device(): summed_time = lax.psum(raw_time, ('src', 'dst'))  100 us
    all_gather x3, blocking collectives, compute_the_numbers(): return jnp.sum(lax.all_gather(local_array, axis_name=bus_axis), axis=0)  74.5 us
    ppermute x18, starting transfers between devices, passed_along(): return lax.ppermute(block, axis, route)  34.4 us
    dot_general x3, matrix products, on_device(): model_cells = jnp.dot(src_now, dst_time, precision=highest)  24.7 us
    dot_general x3, matrix products, on_device(): raw_src = jnp.einsum('ix,rx->ir', residual, dst_time, precision=highest)  17.8 us
    dot_general x3, matrix products, on_device(): raw_dst = jnp.einsum('ijk,rik->jr', resid_cube, src_time, precision=highest)  13.4 us
  transfers between devices with their start and end apart: 18, of which 0 were waited for; matrix products, arithmetic and copies ran while one was open for 6% of the time, Pallas kernels for 0%

profile of v1, /device:TPU:27, one launch (start us, length us, event | category | flops | bytes accessed | tf_op | source)
XLA Modules:
  0.0 463.1 jit_solution(10906123563221120208)
XLA Ops:
  0.7 0.9 slice.72
  1.5 1.3 collective-permute-start
  2.8 0.8 slice.76
  3.7 1.3 collective-permute-start.2
  5.0 1.3 collective-permute-start.3
  6.3 2.1 convert.1
  8.4 1.2 broadcast_multiply_fusion.2
  9.6 8.5 %fusion = f32[64,16384]{1,0:T(8,128)S(1)} fusion(f32[64,64]{1,0:T(8,128)S(1)} %copy-done.4, f32[8,8,128,128]{3,2,1,0:T(8,128)S(1)} %bitcast.89, f32[8,8,128,128]{3,2,1,0:T(8,128)S(1)} %convert.1), kind=kOutput, calls=%fused_computation.3 | convolution fusion | flops 806354944 | bytes 12599296 | tf_op jit(solution)/shard_map/dot_general | solution.py:75
  18.2 6.1 %fusion.7 = f32[64,64]{1,0:T(8,128)S(1)} fusion(f32[64,16384]{1,0:T(8,128)S(1)} %fusion, f32[8,8,128,128]{3,2,1,0:T(8,128)S(1)} %bitcast.90), kind=kOutput, calls=%fused_computation.10 | convolution fusion | flops 805306368 | bytes 8404992 | tf_op jit(solution)/shard_map/ix,rx->ir/dot_general | solution.py:77
  24.3 0.7 copy.9
  25.0 2.9 fusion.31
  28.0 4.5 fusion.28
  32.4 58.2 %psum.42 = f32[128,64]{0,1:T(8,128)S(1)} all-reduce(f32[128,64]{0,1:T(8,128)S(1)} %fusion.28), channel_id=1, replica_groups=mesh['src'=4,'dst'=2,'tm'=4] {'src','tm'}, use_global_device_ids=true, to_apply=%region_1.0 | all-reduce | flops 8192 | bytes 65536 | tf_op jit(solution)/shard_map/psum | solution.py:84
  90.7 24.9 %all-gather = f32[512,64]{1,0:T(8,128)S(1)} all-gather(f32[64,64]{1,0:T(8,128)S(1)} %fusion.7), channel_id=2, replica_groups=mesh['src'=4,'dst'=2,'tm'=4] {'dst','tm'}, dimensions={0}, use_global_device_ids=true | all-gather | bytes 147456 | tf_op jit(solution)/shard_map/all_gather | solution.py:15
  115.8 1.9 collective-permute-start.4
  117.8 4.1 collective-permute-start.1
  121.9 1.3 collective-permute-start.5
  123.2 33.8 %psum.43 = f32[128,64]{0,1:T(8,128)S(1)} all-reduce(f32[128,64]{0,1:T(8,128)S(1)} %fusion.31), channel_id=1, replica_groups=mesh['src'=4,'dst'=2,'tm'=4] {'src','dst'}, use_global_device_ids=true, to_apply=%region_2.0 | all-reduce | flops 8192 | bytes 65536 | tf_op jit(solution)/shard_map/psum | solution.py:85
  157.3 1.2 broadcast_multiply_fusion.1
  159.2 8.1 %convolution_subtract_fusion.1 = f32[64,16384]{1,0:T(8,128)S(1)} fusion(f32[64,64]{1,0:T(8,128)S(1)} %multiply_subtract_fusion.2, f32[8,8,128,128]{3,2,1,0:T(8,128)S(1)} %bitcast.91, f32[8,8,128,128]{3,2,1,0:T(8,128)S(1)} %copy-done.1), kind=kOutput, calls=%fused_computation.1 | convolution fusion | flops 806354944 | bytes 12599296 | tf_op jit(solution)/shard_map/dot_general | solution.py:75
  167.3 5.8 %fusion.4 = f32[64,64]{1,0:T(8,128)S(1)} fusion(f32[64,16384]{1,0:T(8,128)S(1)} %convolution_subtract_fusion.1, f32[8,8,128,128]{3,2,1,0:T(8,128)S(1)} %bitcast.92), kind=kOutput, calls=%fused_computation.7 | convolution fusion | flops 805306368 | bytes 8404992 | tf_op jit(solution)/shard_map/ix,rx->ir/dot_general | solution.py:77
  173.1 0.7 copy.11
  173.9 2.9 fusion.37
  176.8 4.5 fusion.34
  181.3 1.3 collective-permute-start.6
  182.6 1.3 collective-permute-start.8
  183.9 1.3 collective-permute-start.9
  185.2 57.7 %psum.44 = f32[128,64]{0,1:T(8,128)S(1)} all-reduce(f32[128,64]{0,1:T(8,128)S(1)} %fusion.34), channel_id=1, replica_groups=mesh['src'=4,'dst'=2,'tm'=4] {'src','tm'}, use_global_device_ids=true, to_apply=%region_4.5 | all-reduce | flops 8192 | bytes 65536 | tf_op jit(solution)/shard_map/psum | solution.py:84
  242.9 24.7 %all-gather.1 = f32[512,64]{1,0:T(8,128)S(1)} all-gather(f32[64,64]{1,0:T(8,128)S(1)} %fusion.4), channel_id=3, replica_groups=mesh['src'=4,'dst'=2,'tm'=4] {'dst','tm'}, dimensions={0}, use_global_device_ids=true | all-gather | bytes 147456 | tf_op jit(solution)/shard_map/all_gather | solution.py:15
  267.8 1.6 collective-permute-start.10
  269.4 5.0 %collective-permute-start.7 = (f32[1,64]{0,1:T(8,128)S(1)}, f32[1,64]{0,1:T(8,128)S(1)}, u32[]{:S(2)}, u32[]{:S(2)}) collective-permute-start(f32[1,64]{0,1:T(8,128)S(1)} %bitcast.124), channel_id=1, source_target_pairs={{1,0},{2,1},{3,2},{5,4},{6,5},{7,6},{9,8},{10,9},{11,10},{13,12},{... | collective-permute-start | bytes 776 | tf_op jit(solution)/shard_map/ppermute | solution.py:21
  274.4 1.3 collective-permute-start.11
  275.7 33.0 %psum.45 = f32[128,64]{0,1:T(8,128)S(1)} all-reduce(f32[128,64]{0,1:T(8,128)S(1)} %fusion.37), channel_id=1, replica_groups=mesh['src'=4,'dst'=2,'tm'=4] {'src','dst'}, use_global_device_ids=true, to_apply=%region_5.6 | all-reduce | flops 8192 | bytes 65536 | tf_op jit(solution)/shard_map/psum | solution.py:85
  309.0 1.2 broadcast_multiply_fusion
  310.9 8.1 %convolution_subtract_fusion = f32[64,16384]{1,0:T(8,128)S(1)} fusion(f32[8,8,128,128]{3,2,1,0:T(8,128)S(1)} %bitcast.85, f32[8,8,128,128]{3,2,1,0:T(8,128)S(1)} %copy-done.2, f32[64,64]{1,0:T(8,128)S(1)} %multiply_subtract_fusion.2, f32[64,64]{1,0:T(8,128)S(1)} %reduce_sum.28), kind=kOutput, calls=%fused_computation | convolution fusion | flops 806363136 | bytes 12615680 | tf_op jit(solution)/shard_map/dot_general | solution.py:75
  319.0 5.8 %fusion.1 = f32[64,64]{1,0:T(8,128)S(1)} fusion(f32[64,16384]{1,0:T(8,128)S(1)} %convolution_subtract_fusion, f32[8,8,128,128]{3,2,1,0:T(8,128)S(1)} %bitcast.86), kind=kOutput, calls=%fused_computation.4 | convolution fusion | flops 805306368 | bytes 8404992 | tf_op jit(solution)/shard_map/ix,rx->ir/dot_general | solution.py:77
  324.8 0.7 copy.13
  325.5 2.9 fusion.43
  328.5 4.5 fusion.40
  333.0 1.3 collective-permute-start.12
  334.3 1.3 collective-permute-start.14
  335.6 1.3 collective-permute-start.15
  336.9 58.0 %psum.46 = f32[128,64]{0,1:T(8,128)S(1)} all-reduce(f32[128,64]{0,1:T(8,128)S(1)} %fusion.40), channel_id=1, replica_groups=mesh['src'=4,'dst'=2,'tm'=4] {'src','tm'}, use_global_device_ids=true, to_apply=%region_7.8 | all-reduce | flops 8192 | bytes 65536 | tf_op jit(solution)/shard_map/psum | solution.py:84
  395.5 24.9 %all-gather.2 = f32[512,64]{1,0:T(8,128)S(1)} all-gather(f32[64,64]{1,0:T(8,128)S(1)} %fusion.1), channel_id=4, replica_groups=mesh['src'=4,'dst'=2,'tm'=4] {'dst','tm'}, dimensions={0}, use_global_device_ids=true | all-gather | bytes 147456 | tf_op jit(solution)/shard_map/all_gather | solution.py:15
  420.6 1.9 collective-permute-start.16
  423.1 4.4 collective-permute-start.13
  427.5 1.3 collective-permute-start.17
  428.8 33.3 %psum.47 = f32[128,64]{0,1:T(8,128)S(1)} all-reduce(f32[128,64]{0,1:T(8,128)S(1)} %fusion.43), channel_id=1, replica_groups=mesh['src'=4,'dst'=2,'tm'=4] {'src','dst'}, use_global_device_ids=true, to_apply=%region_8.9 | all-reduce | flops 8192 | bytes 65536 | tf_op jit(solution)/shard_map/psum | solution.py:85
  (56 shorter events, 4.7 us)
Async XLA Ops:
  0.6 7.8 %copy-start.3 = (f32[128,64]{0,1:T(8,128)S(1)}, f32[128,64]{0,1:T(8,128)}, u32[]{:S(2)}) copy-start(f32[128,64]{0,1:T(8,128)} %param.7) | copy-start | bytes 98308
  0.6 7.8 %copy-start.5 = (f32[128,64]{0,1:T(8,128)S(1)}, f32[128,64]{0,1:T(8,128)}, u32[]{:S(2)}) copy-start(f32[128,64]{0,1:T(8,128)} %param.6) | copy-start | bytes 98308
  1.5 114.1 %collective-permute-start = (f32[1,64]{0,1:T(8,128)S(1)}, f32[1,64]{0,1:T(8,128)S(1)}, u32[]{:S(2)}, u32[]{:S(2)}) collective-permute-start(f32[1,64]{0,1:T(8,128)S(1)} %slice.72), channel_id=1, source_target_pairs={{0,1},{1,2},{2,3},{4,5},{5,6},{6,7},{8,9},{9,10},{10,11},{12,13},{... | collective-permute-start | bytes 776 | tf_op jit(solution)/shard_map/ppermute | solution.py:21
  3.7 112.0 %collective-permute-start.2 = (f32[32,64]{0,1:T(8,128)S(1)}, f32[32,64]{0,1:T(8,128)S(1)}, u32[]{:S(2)}, u32[]{:S(2)}) collective-permute-start(f32[32,64]{0,1:T(8,128)S(1)} %slice.76), channel_id=1, source_target_pairs={{0,3},{4,7},{8,11},{12,15},{16,19},{20,23},{24,27},{28,31}} | collective-permute-start | bytes 24584 | tf_op jit(solution)/shard_map/ppermute | solution.py:21
  5.0 110.7 %collective-permute-start.3 = (f32[96,64]{0,1:T(8,128)}, f32[96,64]{0,1:T(8,128)S(1)}, u32[]{:S(2)}, u32[]{:S(2)}) collective-permute-start(f32[96,64]{0,1:T(8,128)} %bitcast.104), channel_id=1, source_target_pairs={{0,2},{1,3},{4,6},{5,7},{8,10},{9,11},{12,14},{13,15},{16,18},{17,... | collective-permute-start | bytes 73736 | tf_op jit(solution)/shard_map/ppermute | solution.py:21
  6.3 3.3 copy-start.4
  8.4 9.8 %copy-start = (f32[8,8,128,128]{3,2,1,0:T(8,128)}, f32[8,8,128,128]{3,2,1,0:T(8,128)S(1)}, u32[]{:S(2)}) copy-start(f32[8,8,128,128]{3,2,1,0:T(8,128)S(1)} %convert.1) | copy-start | bytes 12582916
  115.8 41.3 %collective-permute-start.4 = (f32[96,64]{0,1:T(8,128)S(1)}, f32[96,64]{0,1:T(8,128)S(1)}, u32[]{:S(2)}, u32[]{:S(2)}) collective-permute-start(f32[96,64]{0,1:T(8,128)S(1)} %slice.98), channel_id=1, source_target_pairs={{2,0},{3,1},{6,4},{7,5},{10,8},{11,9},{14,12},{15,13},{18,16},{19,... | collective-permute-start | bytes 73736 | tf_op jit(solution)/shard_map/ppermute | solution.py:21
  117.8 39.3 %collective-permute-start.1 = (f32[1,64]{0,1:T(8,128)S(1)}, f32[1,64]{0,1:T(8,128)S(1)}, u32[]{:S(2)}, u32[]{:S(2)}) collective-permute-start(f32[1,64]{0,1:T(8,128)S(1)} %bitcast.122), channel_id=1, source_target_pairs={{1,0},{2,1},{3,2},{5,4},{6,5},{7,6},{9,8},{10,9},{11,10},{13,12},{... | collective-permute-start | bytes 776 | tf_op jit(solution)/shard_map/ppermute | solution.py:21
  121.9 35.2 %collective-permute-start.5 = (f32[32,64]{0,1:T(8,128)S(1)}, f32[32,64]{0,1:T(8,128)S(1)}, u32[]{:S(2)}, u32[]{:S(2)}) collective-permute-start(f32[32,64]{0,1:T(8,128)S(1)} %bitcast.121), channel_id=1, source_target_pairs={{3,0},{7,4},{11,8},{15,12},{19,16},{23,20},{27,24},{31,28}} | collective-permute-start | bytes 24584 | tf_op jit(solution)/shard_map/ppermute | solution.py:21
  157.0 2.2 copy-start.1
  181.3 86.3 %collective-permute-start.6 = (f32[1,64]{0,1:T(8,128)S(1)}, f32[1,64]{0,1:T(8,128)S(1)}, u32[]{:S(2)}, u32[]{:S(2)}) collective-permute-start(f32[1,64]{0,1:T(8,128)S(1)} %slice.100), channel_id=1, source_target_pairs={{0,1},{1,2},{2,3},{4,5},{5,6},{6,7},{8,9},{9,10},{10,11},{12,13},{... | collective-permute-start | bytes 776 | tf_op jit(solution)/shard_map/ppermute | solution.py:21
  182.6 85.0 %collective-permute-start.8 = (f32[32,64]{0,1:T(8,128)S(1)}, f32[32,64]{0,1:T(8,128)S(1)}, u32[]{:S(2)}, u32[]{:S(2)}) collective-permute-start(f32[32,64]{0,1:T(8,128)S(1)} %slice.104), channel_id=1, source_target_pairs={{0,3},{4,7},{8,11},{12,15},{16,19},{20,23},{24,27},{28,31}} | collective-permute-start | bytes 24584 | tf_op jit(solution)/shard_map/ppermute | solution.py:21
  183.9 83.8 %collective-permute-start.9 = (f32[96,64]{0,1:T(8,128)S(1)}, f32[96,64]{0,1:T(8,128)S(1)}, u32[]{:S(2)}, u32[]{:S(2)}) collective-permute-start(f32[96,64]{0,1:T(8,128)S(1)} %bitcast.101), channel_id=1, source_target_pairs={{0,2},{1,3},{4,6},{5,7},{8,10},{9,11},{12,14},{13,15},{16,18},{17,... | collective-permute-start | bytes 73736 | tf_op jit(solution)/shard_map/ppermute | solution.py:21
  267.8 40.9 %collective-permute-start.10 = (f32[96,64]{0,1:T(8,128)S(1)}, f32[96,64]{0,1:T(8,128)S(1)}, u32[]{:S(2)}, u32[]{:S(2)}) collective-permute-start(f32[96,64]{0,1:T(8,128)S(1)} %slice.106), channel_id=1, source_target_pairs={{2,0},{3,1},{6,4},{7,5},{10,8},{11,9},{14,12},{15,13},{18,16},{19,... | collective-permute-start | bytes 73736 | tf_op jit(solution)/shard_map/ppermute | solution.py:21
  269.4 39.3 %collective-permute-start.7 = (f32[1,64]{0,1:T(8,128)S(1)}, f32[1,64]{0,1:T(8,128)S(1)}, u32[]{:S(2)}, u32[]{:S(2)}) collective-permute-start(f32[1,64]{0,1:T(8,128)S(1)} %bitcast.124), channel_id=1, source_target_pairs={{1,0},{2,1},{3,2},{5,4},{6,5},{7,6},{9,8},{10,9},{11,10},{13,12},{... | collective-permute-start | bytes 776 | tf_op jit(solution)/shard_map/ppermute | solution.py:21
  274.4 34.3 %collective-permute-start.11 = (f32[32,64]{0,1:T(8,128)S(1)}, f32[32,64]{0,1:T(8,128)S(1)}, u32[]{:S(2)}, u32[]{:S(2)}) collective-permute-start(f32[32,64]{0,1:T(8,128)S(1)} %bitcast.123), channel_id=1, source_target_pairs={{3,0},{7,4},{11,8},{15,12},{19,16},{23,20},{27,24},{31,28}} | collective-permute-start | bytes 24584 | tf_op jit(solution)/shard_map/ppermute | solution.py:21
  308.7 2.2 copy-start.2
  333.0 87.5 %collective-permute-start.12 = (f32[1,64]{0,1:T(8,128)S(1)}, f32[1,64]{0,1:T(8,128)S(1)}, u32[]{:S(2)}, u32[]{:S(2)}) collective-permute-start(f32[1,64]{0,1:T(8,128)S(1)} %slice.108), channel_id=1, source_target_pairs={{0,1},{1,2},{2,3},{4,5},{5,6},{6,7},{8,9},{9,10},{10,11},{12,13},{... | collective-permute-start | bytes 776 | tf_op jit(solution)/shard_map/ppermute | solution.py:21
  334.3 86.2 %collective-permute-start.14 = (f32[32,64]{0,1:T(8,128)S(1)}, f32[32,64]{0,1:T(8,128)S(1)}, u32[]{:S(2)}, u32[]{:S(2)}) collective-permute-start(f32[32,64]{0,1:T(8,128)S(1)} %slice.112), channel_id=1, source_target_pairs={{0,3},{4,7},{8,11},{12,15},{16,19},{20,23},{24,27},{28,31}} | collective-permute-start | bytes 24584 | tf_op jit(solution)/shard_map/ppermute | solution.py:21
  335.6 84.9 %collective-permute-start.15 = (f32[96,64]{0,1:T(8,128)S(1)}, f32[96,64]{0,1:T(8,128)S(1)}, u32[]{:S(2)}, u32[]{:S(2)}) collective-permute-start(f32[96,64]{0,1:T(8,128)S(1)} %bitcast.110), channel_id=1, source_target_pairs={{0,2},{1,3},{4,6},{5,7},{8,10},{9,11},{12,14},{13,15},{16,18},{17,... | collective-permute-start | bytes 73736 | tf_op jit(solution)/shard_map/ppermute | solution.py:21
  420.6 41.6 %collective-permute-start.16 = (f32[96,64]{0,1:T(8,128)S(1)}, f32[96,64]{0,1:T(8,128)S(1)}, u32[]{:S(2)}, u32[]{:S(2)}) collective-permute-start(f32[96,64]{0,1:T(8,128)S(1)} %slice.114), channel_id=1, source_target_pairs={{2,0},{3,1},{6,4},{7,5},{10,8},{11,9},{14,12},{15,13},{18,16},{19,... | collective-permute-start | bytes 73736 | tf_op jit(solution)/shard_map/ppermute | solution.py:21
  423.1 39.1 %collective-permute-start.13 = (f32[1,64]{0,1:T(8,128)S(1)}, f32[1,64]{0,1:T(8,128)S(1)}, u32[]{:S(2)}, u32[]{:S(2)}) collective-permute-start(f32[1,64]{0,1:T(8,128)S(1)} %bitcast.126), channel_id=1, source_target_pairs={{1,0},{2,1},{3,2},{5,4},{6,5},{7,6},{9,8},{10,9},{11,10},{13,12},{... | collective-permute-start | bytes 776 | tf_op jit(solution)/shard_map/ppermute | solution.py:21
  427.5 34.7 %collective-permute-start.17 = (f32[32,64]{0,1:T(8,128)S(1)}, f32[32,64]{0,1:T(8,128)S(1)}, u32[]{:S(2)}, u32[]{:S(2)}) collective-permute-start(f32[32,64]{0,1:T(8,128)S(1)} %bitcast.125), channel_id=1, source_target_pairs={{3,0},{7,4},{11,8},{15,12},{19,16},{23,20},{27,24},{31,28}} | collective-permute-start | bytes 24584 | tf_op jit(solution)/shard_map/ppermute | solution.py:21
